TPU v7x, 256 devices: a whole 4x4x8 slice. The times are simulated.
256 devices in a mesh: dp: 32 (over y_hi, z, core), shard: 8 (over x, y_lo).
Axes of the slice: x: 4, y: 4 (y_hi: 2, y_lo: 2; y = y_hi * 2 + y_lo), z: 8, core: 2. Of those that a mesh axis runs over, the one named last changes fastest.
Arguments:
- resid_in: bfloat16 [4096, 8192], P('dp', 'shard'), may hold values from -6 to 6
- hidden: bfloat16 [4096, 28672], P('shard', 'dp'), may hold values from -6 to 6
- w_down: bfloat16 [28672, 8192], P('dp', 'shard'), may hold values from -0.03125 to 0.03125
- frozen: bfloat16 [4096, 8192], P(('dp', 'shard')), may hold values from -6 to 6
- steer: bfloat16 [8192], P('shard'), may hold values from -6 to 6
- forget_flags: int32 [16], replicated, may hold values from 0 to 1, as said below
Outputs:
- updated: bfloat16 [4096, 8192], P('dp', 'shard')
- grad_down: float32 [28672, 8192], P('dp', 'shard')
Inputs may be any that keep to these rules, and one draw needn't show every extreme that they name: `forget_flags`: exactly half of the 16 sequences are forget sequences.
All inputs are finite; a program needn't handle non-finite values.
Results may differ from a plain program's by a relative error of at most 0.0019.
Values may be sent and summed in bfloat16 or wider, within the bound.
A program may use at most 128 MiB of HBM per device.

v0:
```python
import math
import jax
import jax.numpy as jnp
from jax import lax
from jax.sharding import Mesh, PartitionSpec as P

SEQ_LEN = 256
retain_weight = 2.0


def per_device(resid_in, hidden, w_down, frozen, steer, forget_flags):
    n_c = lax.axis_size("c")
    tok_rows, d_cols = resid_in.shape
    ff_rows = w_down.shape[0]
    whole_hidden = lax.all_gather(hidden, "shard", axis=0, tiled=True)
    total_tokens = whole_hidden.shape[0]
    wh = whole_hidden.reshape(n_c, 2, tok_rows, ff_rows)
    swapped = lax.all_to_all(wh, "core", split_axis=1, concat_axis=1, tiled=True)
    mine = jnp.transpose(swapped, (0, 2, 1, 3)).reshape(n_c * tok_rows, 2 * ff_rows)
    pair_w = lax.all_gather(w_down, "core", axis=0, tiled=True)
    partial = jnp.dot(mine, pair_w, preferred_element_type=jnp.float32)
    mlp_out = lax.psum_scatter(partial, "c", scatter_dimension=0, tiled=True)
    residual = resid_in.astype(jnp.float32) + mlp_out
    updated = residual.astype(jnp.bfloat16)
    target_rows = lax.all_to_all(frozen, "shard", split_axis=1, concat_axis=0, tiled=True)
    row_block = lax.axis_index("c") * 2 + lax.axis_index("core")
    start_row = row_block * tok_rows
    seq_ids = (start_row + jnp.arange(tok_rows, dtype=jnp.int32)) // SEQ_LEN
    seq_match = seq_ids[:, None] == jnp.arange(forget_flags.shape[0], dtype=jnp.int32)[None, :]
    is_forget = jnp.sum(jnp.where(seq_match, forget_flags[None, :], 0), axis=1) > 0
    target = jnp.where(
        is_forget[:, None], steer.astype(jnp.float32)[None, :], target_rows.astype(jnp.float32)
    )
    loss_weight = jnp.where(is_forget, 1.0, retain_weight).astype(jnp.float32)
    slopes = (loss_weight[:, None] * (residual - target) * (1.0 / math.sqrt(total_tokens))).astype(
        jnp.bfloat16
    )
    half_slopes = lax.all_gather(slopes, "c", axis=0, tiled=False)
    all_slopes = lax.all_gather(half_slopes, "core", axis=0, tiled=False)
    grad_down = jnp.einsum("mptf,pmtd->fd", wh, all_slopes, preferred_element_type=jnp.float32)
    return (updated, grad_down)


def solution(mesh):
    n_dp, n_shard = mesh.devices.shape
    pair_mesh = Mesh(mesh.devices.reshape(n_dp // 2, 2, n_shard), ("c", "core", "shard"))
    dp = ("c", "core")
    in_specs = (
        P(dp, "shard"),
        P("shard", dp),
        P(dp, "shard"),
        P(("c", "core", "shard"), None),
        P("shard"),
        P(),
    )
    out_specs = (P(dp, "shard"), P(dp, "shard"))
    return jax.shard_map(
        per_device, mesh=pair_mesh, in_specs=in_specs, out_specs=out_specs, check_vma=False
    )
```

profile of v0, /device:TPU:1, one launch (start us, length us, event | category | flops | bytes accessed | tf_op | source)
XLA Modules:
  0.0 582.2 jit_solution(232954384777330829)
XLA Ops:
  7.2 0.0 all-gather.7.cloned.1.call-start
  7.2 0.7 all-gather.7.cloned.1.call-update
  7.9 0.0 all-gather.9.cloned.1.call-start
  7.9 0.7 all-gather.9.cloned.1.call-update
  8.6 0.0 reduce-scatter.2.cloned.1.call-start
  8.7 156.2 %all-gather.7.cloned.1.call-done = bf16[4096,896]{1,0:T(8,128)(2,1)} async-done(((bf16[512,896]{1,0:T(8,128)(2,1)}), bf16[4096,896]{1,0:T(8,128)(2,1)}) %all-gather.7.cloned.1.call-update) | async-done | bytes 7340048 | tf_op jit(solution)/shard_map/all_gather | solution.py:15
  164.9 4.0 copy.19
  168.9 11.2 %all_to_all.18 = bf16[16,2,128,896]{3,2,0,1:T(8,128)(2,1)} all-to-all(bf16[16,2,128,896]{3,2,0,1:T(8,128)(2,1)S(1)} %copy.19), channel_id=1, replica_groups=mesh['c'=16,'core'=2,'shard'=8] {'core'}, dimensions={1} | all-to-all | bytes 14680064 | tf_op jit(solution)/shard_map/all_to_all | solution.py:18
  180.1 12.3 %copy.20 = bf16[16,128,2,896]{1,0,3,2:T(8,128)(2,1)} copy(bf16[16,128,2,896]{3,1,0,2:T(8,128)(2,1)} %bitcast.35) | data formatting | bytes 14680064 | tf_op jit(solution)/shard_map/transpose | solution.py:19
  192.4 0.0 all-gather.9.cloned.1.call-done
  192.4 13.2 %fusion.2 = f32[2048,1024]{1,0:T(8,128)} fusion(bf16[1792,1024]{1,0:T(8,128)(2,1)} %all-gather.9.cloned.1.call-done, bf16[224,8,16,128]{3,2,1,0:T(8,128)(2,1)} %bitcast.38), kind=kOutput, calls=%fused_computation.2 | convolution fusion | flops 7516192768 | bytes 19398656 | tf_op jit(solution)/shard_map/dot_general | solution.py:21
  205.6 0.0 copy-start
  205.6 0.0 copy-start.3
  205.6 0.0 copy-start.2
  205.6 0.0 copy-start.1
  205.7 0.0 reduce-scatter.2.cloned.1.call-update
  205.7 0.9 copy-done
  206.6 0.7 copy.38
  207.3 7.0 %all-to-all-start.1 = ((bf16[16,8,1024]{2,0,1:T(8,128)(2,1)}), bf16[16,8,1024]{2,0,1:T(8,128)(2,1)S(1)}, u32[]{:S(2)}, u32[]{:S(2)}) async-start(bf16[16,8,1024]{2,0,1:T(8,128)(2,1)} %bitcast.34), calls=%async_computation.2 | async-start | bytes 524288 | tf_op jit(solution)/shard_map/all_to_all | solution.py:25
  214.3 0.0 all-gather.11.cloned.1.call-start
  214.4 0.0 copy-done.3
  214.4 0.1 select_reduce_fusion
  214.5 0.0 copy-done.2
  214.5 5.7 all-to-all-done.1
  220.2 206.1 %reduce-scatter.2.cloned.1.call-done = f32[128,1024]{1,0:T(8,128)} async-done(((f32[2048,1024]{1,0:T(8,128)}), f32[128,1024]{1,0:T(8,128)}) %reduce-scatter.2.cloned.1.call-update) | async-done | bytes 524304 | tf_op jit(solution)/shard_map/reduce_scatter | solution.py:22
  426.4 0.0 copy-done.1
  426.4 2.0 fusion.11
  428.4 0.0 all-gather.11.cloned.1.call-update
  428.4 0.0 all-gather.13.cloned.1.call-start
  428.4 100.3 %all-gather.11.cloned.1.call-done = bf16[2048,1024]{1,0:T(8,128)(2,1)} async-done(((bf16[128,1024]{1,0:T(8,128)(2,1)}), bf16[2048,1024]{1,0:T(8,128)(2,1)}) %all-gather.11.cloned.1.call-update) | async-done | bytes 4194320 | tf_op jit(solution)/shard_map/all_gather | solution.py:38
  528.7 0.0 all-gather.13.cloned.1.call-update
  528.8 27.3 %all-gather.13.cloned.1.call-done = bf16[32,128,1024]{2,1,0:T(8,128)(2,1)} async-done(((bf16[16,128,1024]{2,1,0:T(8,128)(2,1)}), bf16[32,128,1024]{2,1,0:T(8,128)(2,1)}) %all-gather.13.cloned.1.call-update) | async-done | bytes 8388624 | tf_op jit(solution)/shard_map/all_gather | solution.py:39
  556.1 14.6 %fusion.5 = f32[896,1024]{0,1:T(8,128)} fusion(bf16[16,2,128,896]{3,2,1,0:T(8,128)(2,1)} %bitcast.37, bf16[2,16,128,1024]{3,2,1,0:T(8,128)(2,1)} %bitcast.41), kind=kOutput, calls=%fused_computation.5 | convolution fusion | flops 7516192768 | bytes 19398656 | tf_op jit(solution)/shard_map/mptf,pmtd->fd/dot_general | solution.py:40
  570.7 5.0 copy.23
  (4 shorter events, 0.0 us)
Async XLA Ops:
  7.2 157.7 %all-gather.7.cloned.1.call-start = ((), (), s32[]{:S(2)}) async-start(), calls=%async_computation.3 | async-start | bytes 8257536 | tf_op jit(solution)/shard_map/all_gather | solution.py:15
  7.9 184.5 %all-gather.9.cloned.1.call-start = ((), (), s32[]{:S(2)}) async-start(), calls=%async_computation.4 | async-start | bytes 5505024 | tf_op jit(solution)/shard_map/all_gather | solution.py:20
  8.6 417.7 %reduce-scatter.2.cloned.1.call-start = ((), (), s32[]{:S(2)}) async-start(), calls=%async_computation.5 | async-start | bytes 8912896 | tf_op jit(solution)/shard_map/reduce_scatter | solution.py:22
  205.6 0.9 copy-start
  205.6 8.7 %copy-start.3 = (s32[16]{0:T(128)S(1)}, s32[16]{0:T(128)}, u32[]{:S(2)}) copy-start(s32[16]{0:T(128)} %param.11) | copy-start | bytes 196
  205.6 8.8 %copy-start.2 = (bf16[1024]{0:T(1024)(128)(2,1)S(1)}, bf16[1024]{0:T(1024)(128)(2,1)}, u32[]{:S(2)}) copy-start(bf16[1024]{0:T(1024)(128)(2,1)} %param.10) | copy-start | bytes 6148
  205.6 220.7 %copy-start.1 = (bf16[128,1024]{1,0:T(8,128)(2,1)S(1)}, bf16[128,1024]{1,0:T(8,128)(2,1)}, u32[]{:S(2)}) copy-start(bf16[128,1024]{1,0:T(8,128)(2,1)} %param.6) | copy-start | bytes 786436
  207.3 12.9 %all-to-all-start.1 = ((bf16[16,8,1024]{2,0,1:T(8,128)(2,1)}), bf16[16,8,1024]{2,0,1:T(8,128)(2,1)S(1)}, u32[]{:S(2)}, u32[]{:S(2)}) async-start(bf16[16,8,1024]{2,0,1:T(8,128)(2,1)} %bitcast.34), calls=%async_computation.2 | async-start | bytes 524288 | tf_op jit(solution)/shard_map/all_to_all | solution.py:25
  214.3 314.4 %all-gather.11.cloned.1.call-start = ((), (), s32[]{:S(2)}) async-start(), calls=%async_computation.6 | async-start | bytes 4456448 | tf_op jit(solution)/shard_map/all_gather | solution.py:38
  428.4 127.7 %all-gather.13.cloned.1.call-start = ((), (), s32[]{:S(2)}) async-start(), calls=%async_computation.7 | async-start | bytes 12582912 | tf_op jit(solution)/shard_map/all_gather | solution.py:39
Sparse Core Ops, SparseCore 0:
  9.8 155.0 all-gather.6
  166.6 21.0 all-gather.8
  205.8 220.5 reduce-scatter.1
  429.4 99.3 all-gather.10
  530.4 25.6 all-gather.12
where the time goes:
time: 583 us; the launch traced here: 582 us
  waiting for transfers between devices  497 us (85%)
  matrix products  27.9 us (5%)
  local copies, waits for them, and re-layouts  23 us (4%)
  between operations  13.8 us (2%)
  blocking collectives  11.2 us (2%)
  starting transfers between devices  7.19 us (1%)
    reduce_scatter x1, waiting for transfers between devices, per_device(): mlp_out = lax.psum_scatter(partial, 'c', scatter_dimension=0, tiled=True)  206 us
    all_gather x1, waiting for transfers between devices, per_device(): whole_hidden = lax.all_gather(hidden, 'shard', axis=0, tiled=True)  156 us
    all_gather x1, waiting for transfers between devices, per_device(): half_slopes = lax.all_gather(slopes, 'c', axis=0, tiled=False)  100 us
    all_gather x1, waiting for transfers between devices, per_device(): all_slopes = lax.all_gather(half_slopes, 'core', axis=0, tiled=False)  27.3 us
    dot_general x1, matrix products, per_device(): jnp.einsum('mptf,pmtd->fd', wh, all_slopes, preferred_element_type=jnp.fl...  14.6 us
    dot_general x1, matrix products, per_device(): partial = jnp.dot(mine, pair_w, preferred_element_type=jnp.float32)  13.2 us
    transpose x1, local copies, waits for them, and re-layouts, per_device(): jnp.transpose(swapped, (0, 2, 1, 3)).reshape(n_c * tok_rows, 2 * ff_rows)  12.3 us
  transfers between devices with their start and end apart: 6, of which 5 were waited for; matrix products, arithmetic and copies ran while one was open for 3% of the time, Pallas kernels for 0%

commit v1 on v0

--- a/solution.py
+++ b/solution.py
@@ -8,11 +8,16 @@
 retain_weight = 2.0
 
 
+def all_by_exchange(shard, name, dim):
+    repeated = jnp.stack([shard] * lax.axis_size(name))
+    return jnp.concatenate(lax.all_to_all(repeated, name, 0, 0), axis=dim)
+
+
 def per_device(resid_in, hidden, w_down, frozen, steer, forget_flags):
     n_c = lax.axis_size("c")
     tok_rows, d_cols = resid_in.shape
     ff_rows = w_down.shape[0]
-    whole_hidden = lax.all_gather(hidden, "shard", axis=0, tiled=True)
+    whole_hidden = all_by_exchange(hidden, "shard", 0)
     total_tokens = whole_hidden.shape[0]
     wh = whole_hidden.reshape(n_c, 2, tok_rows, ff_rows)
     swapped = lax.all_to_all(wh, "core", split_axis=1, concat_axis=1, tiled=True)

time: 583 us -> 538 us (0.923)
  waiting for transfers between devices: 497 us -> 443 us
    all_gather x1 -> x0, waiting for transfers between devices: 156 us -> none  [per_device(): whole_hidden = lax.all_gather(hidden, 'shard', axis=0, tiled=True)]
    all_to_all x0 -> x1, waiting for transfers between devices: none -> 99.7 us  [all_by_exchange(): return jnp.concatenate(lax.all_to_all(repeated, name, 0, 0), axis=dim)]
    another operation x0 -> x2, local copies, waits for them, and re-layouts: none -> 9.09 us  [the longest x1 5.06 us: all_by_exchange(): repeated = jnp.stack([shard] * lax.axis_size(name))]
    all_to_all x0 -> x1, starting transfers between devices: none -> 5.86 us  [all_by_exchange(): return jnp.concatenate(lax.all_to_all(repeated, name, 0, 0), axis=dim)]
where the time goes in v1:
time: 538 us; the launch traced here: 537 us
  waiting for transfers between devices  443 us (82%)
  local copies, waits for them, and re-layouts  27.8 us (5%)
  matrix products  27.8 us (5%)
  between operations  13.8 us (3%)
  blocking collectives  12.7 us (2%)
  starting transfers between devices  9.43 us (2%)
    reduce_scatter x1, waiting for transfers between devices, per_device(): mlp_out = lax.psum_scatter(partial, 'c', scatter_dimension=0, tiled=True)  209 us
    all_gather x1, waiting for transfers between devices, per_device(): half_slopes = lax.all_gather(slopes, 'c', axis=0, tiled=False)  100 us
    all_to_all x1, waiting for transfers between devices, all_by_exchange(): return jnp.concatenate(lax.all_to_all(repeated, name, 0, 0), axis=dim)  99.7 us
    all_gather x1, waiting for transfers between devices, per_device(): all_slopes = lax.all_gather(half_slopes, 'core', axis=0, tiled=False)  27.3 us
    dot_general x1, matrix products, per_device(): jnp.einsum('mptf,pmtd->fd', wh, all_slopes, preferred_element_type=jnp.fl...  14.6 us
    dot_general x1, matrix products, per_device(): partial = jnp.dot(mine, pair_w, preferred_element_type=jnp.float32)  13.2 us
    all_to_all x1, blocking collectives, per_device(): lax.all_to_all(wh, 'core', split_axis=1, concat_axis=1, tiled=True)  12.7 us
    transpose x1, local copies, waits for them, and re-layouts, per_device(): jnp.transpose(swapped, (0, 2, 1, 3)).reshape(n_c * tok_rows, 2 * ff_rows)  12 us
  transfers between devices with their start and end apart: 6, of which 5 were waited for; matrix products, arithmetic and copies ran while one was open for 3% of the time, Pallas kernels for 0%

profile of v1, /device:TPU:1, one launch (start us, length us, event | category | flops | bytes accessed | tf_op | source)
XLA Modules:
  0.0 536.7 jit_solution(18020133830291922775)
XLA Ops:
  7.2 5.1 stack.2
  12.2 5.9 %all-to-all-start = ((bf16[8,512,896]{2,1,0:T(8,128)(2,1)}), bf16[8,512,896]{2,1,0:T(8,128)(2,1)}, u32[]{:S(2)}, u32[]{:S(2)}) async-start(bf16[8,512,896]{2,1,0:T(8,128)(2,1)} %stack.2), calls=%async_computation | async-start | bytes 14680064 | tf_op jit(solution)/shard_map/all_to_all | solution.py:13
  18.1 0.0 all-gather.6.cloned.1.call-start
  18.1 0.7 all-gather.6.cloned.1.call-update
  18.8 0.0 reduce-scatter.2.cloned.1.call-start
  18.9 99.7 %all-to-all-done = bf16[8,512,896]{2,1,0:T(8,128)(2,1)} async-done(((bf16[8,512,896]{2,1,0:T(8,128)(2,1)}), bf16[8,512,896]{2,1,0:T(8,128)(2,1)}, u32[]{:S(2)}, u32[]{:S(2)}) %all-to-all-start) | async-done | bytes 7340064 | tf_op jit(solution)/shard_map/all_to_all | solution.py:13
  118.5 4.0 copy.19
  122.6 12.7 %all_to_all.23 = bf16[16,2,128,896]{3,2,0,1:T(8,128)(2,1)} all-to-all(bf16[16,2,128,896]{3,2,0,1:T(8,128)(2,1)S(1)} %copy.19), channel_id=1, replica_groups=mesh['c'=16,'core'=2,'shard'=8] {'core'}, dimensions={1} | all-to-all | bytes 14680064 | tf_op jit(solution)/shard_map/all_to_all | solution.py:23
  135.3 12.0 %copy.20 = bf16[16,128,2,896]{1,0,3,2:T(8,128)(2,1)} copy(bf16[16,128,2,896]{3,1,0,2:T(8,128)(2,1)} %bitcast.35) | data formatting | bytes 14680064 | tf_op jit(solution)/shard_map/transpose | solution.py:24
  147.4 0.0 all-gather.6.cloned.1.call-done
  147.4 13.2 %fusion.2 = f32[2048,1024]{1,0:T(8,128)} fusion(bf16[1792,1024]{1,0:T(8,128)(2,1)} %all-gather.6.cloned.1.call-done, bf16[224,8,16,128]{3,2,1,0:T(8,128)(2,1)} %bitcast.36), kind=kOutput, calls=%fused_computation.2 | convolution fusion | flops 7516192768 | bytes 19398656 | tf_op jit(solution)/shard_map/dot_general | solution.py:26
  160.6 0.0 copy-start
  160.6 0.0 copy-start.3
  160.6 0.0 copy-start.2
  160.6 0.0 copy-start.1
  160.6 0.0 reduce-scatter.2.cloned.1.call-update
  160.6 0.9 copy-done
  161.5 0.7 copy.38
  162.2 3.4 all-to-all-start.2
  165.7 0.0 all-gather.8.cloned.1.call-start
  165.7 0.0 copy-done.3
  165.8 0.1 select_reduce_fusion
  165.8 0.0 copy-done.2
  165.9 6.3 %all-to-all-done.2 = bf16[16,8,1024]{2,0,1:T(8,128)(2,1)S(1)} async-done(((bf16[16,8,1024]{2,0,1:T(8,128)(2,1)}), bf16[16,8,1024]{2,0,1:T(8,128)(2,1)S(1)}, u32[]{:S(2)}, u32[]{:S(2)}) %all-to-all-start.2) | async-done | bytes 262176 | tf_op jit(solution)/shard_map/all_to_all | solution.py:30
  172.1 208.7 %reduce-scatter.2.cloned.1.call-done = f32[128,1024]{1,0:T(8,128)} async-done(((f32[2048,1024]{1,0:T(8,128)}), f32[128,1024]{1,0:T(8,128)}) %reduce-scatter.2.cloned.1.call-update) | async-done | bytes 524304 | tf_op jit(solution)/shard_map/reduce_scatter | solution.py:27
  380.8 0.0 copy-done.1
  380.8 2.0 fusion.11
  382.8 0.0 all-gather.8.cloned.1.call-update
  382.9 0.0 all-gather.10.cloned.1.call-start
  382.9 100.4 %all-gather.8.cloned.1.call-done = bf16[2048,1024]{1,0:T(8,128)(2,1)} async-done(((bf16[128,1024]{1,0:T(8,128)(2,1)}), bf16[2048,1024]{1,0:T(8,128)(2,1)}) %all-gather.8.cloned.1.call-update) | async-done | bytes 4194320 | tf_op jit(solution)/shard_map/all_gather | solution.py:43
  483.3 0.0 all-gather.10.cloned.1.call-update
  483.3 27.3 %all-gather.10.cloned.1.call-done = bf16[32,128,1024]{2,1,0:T(8,128)(2,1)} async-done(((bf16[16,128,1024]{2,1,0:T(8,128)(2,1)}), bf16[32,128,1024]{2,1,0:T(8,128)(2,1)}) %all-gather.10.cloned.1.call-update) | async-done | bytes 8388624 | tf_op jit(solution)/shard_map/all_gather | solution.py:44
  510.6 14.6 %fusion.5 = f32[896,1024]{0,1:T(8,128)} fusion(bf16[16,2,128,896]{3,2,1,0:T(8,128)(2,1)} %bitcast, bf16[2,16,128,1024]{3,2,1,0:T(8,128)(2,1)} %bitcast.39), kind=kOutput, calls=%fused_computation.5 | convolution fusion | flops 7516192768 | bytes 19398656 | tf_op jit(solution)/shard_map/mptf,pmtd->fd/dot_general | solution.py:45
  525.2 5.0 copy.23
  (4 shorter events, 0.0 us)
Async XLA Ops:
  12.2 106.3 %all-to-all-start = ((bf16[8,512,896]{2,1,0:T(8,128)(2,1)}), bf16[8,512,896]{2,1,0:T(8,128)(2,1)}, u32[]{:S(2)}, u32[]{:S(2)}) async-start(bf16[8,512,896]{2,1,0:T(8,128)(2,1)} %stack.2), calls=%async_computation | async-start | bytes 14680064 | tf_op jit(solution)/shard_map/all_to_all | solution.py:13
  18.1 129.3 %all-gather.6.cloned.1.call-start = ((), (), s32[]{:S(2)}) async-start(), calls=%async_computation.4 | async-start | bytes 5505024 | tf_op jit(solution)/shard_map/all_gather | solution.py:25
  18.8 362.0 %reduce-scatter.2.cloned.1.call-start = ((), (), s32[]{:S(2)}) async-start(), calls=%async_computation.5 | async-start | bytes 8912896 | tf_op jit(solution)/shard_map/reduce_scatter | solution.py:27
  160.6 0.9 copy-start
  160.6 5.2 copy-start.3
  160.6 5.3 copy-start.2
  160.6 220.2 %copy-start.1 = (bf16[128,1024]{1,0:T(8,128)(2,1)S(1)}, bf16[128,1024]{1,0:T(8,128)(2,1)}, u32[]{:S(2)}) copy-start(bf16[128,1024]{1,0:T(8,128)(2,1)} %param.6) | copy-start | bytes 786436
  162.2 9.9 %all-to-all-start.2 = ((bf16[16,8,1024]{2,0,1:T(8,128)(2,1)}), bf16[16,8,1024]{2,0,1:T(8,128)(2,1)S(1)}, u32[]{:S(2)}, u32[]{:S(2)}) async-start(bf16[16,8,1024]{2,0,1:T(8,128)(2,1)} %bitcast.34), calls=%async_computation.3 | async-start | bytes 524288 | tf_op jit(solution)/shard_map/all_to_all | solution.py:30
  165.7 317.6 %all-gather.8.cloned.1.call-start = ((), (), s32[]{:S(2)}) async-start(), calls=%async_computation.6 | async-start | bytes 4456448 | tf_op jit(solution)/shard_map/all_gather | solution.py:43
  382.9 127.7 %all-gather.10.cloned.1.call-start = ((), (), s32[]{:S(2)}) async-start(), calls=%async_computation.7 | async-start | bytes 12582912 | tf_op jit(solution)/shard_map/all_gather | solution.py:44
Sparse Core Ops, SparseCore 0:
  20.7 22.3 all-gather.5
  160.7 220.0 reduce-scatter.1
  384.0 99.2 all-gather.7
  484.9 25.6 all-gather.9
